TPU v7x, 32 devices: a whole 2x2x4 slice. The times are simulated.
32 devices in a mesh: expert: 8 (over z, y), etp: 4 (over x, core).
Axes of the slice: x: 2, y: 2, z: 4, core: 2. Of those that a mesh axis runs over, the one named last changes fastest.
Arguments:
- tokens: bfloat16 [4096, 2560], P(('expert', 'etp')), may hold values from -6 to 6
- hidden_grad: bfloat16 [4096, 4096], P(('expert', 'etp')), may hold values from -6 to 6
- routes: int32 [4096, 1], P(('expert', 'etp')), may hold values from 0 to 7; in each aligned block of 512 rows (0 to 511, 512 to 1023, ...) at most 80 rows name the same one
- exponents: int32 [4096], P(('expert', 'etp')), may hold values from -2 to 2
- gate_weight: bfloat16 [8, 2560, 4096], P('expert', None, 'etp'), may hold values from -0.125 to 0.125
- up_weight: bfloat16 [8, 2560, 4096], P('expert', None, 'etp'), may hold values from -0.125 to 0.125
Outputs:
- input_grad: bfloat16 [4096, 2560], P(('expert', 'etp'))
Inputs may be any that keep to these rules, and one draw needn't show every extreme that they name: `routes`: in each aligned block of 512 rows (the tokens of one group of devices along etp) no expert is named by more than 80 rows, and in every draw some expert is named by exactly 80 rows of some block.
All inputs are finite; a program needn't handle non-finite values.
Results may differ from a plain program's by a relative error of at most 0.0095.
Values may be sent and summed in bfloat16 or wider, within the bound.
A program may use at most 128 MiB of HBM per device.

v0:
```python
import jax
import jax.numpy as jnp
from jax import lax
from jax.sharding import PartitionSpec as P


def on_device(tokens, hidden_grad, routes, exponents, gate_weight, up_weight):
    feature_count = tokens.shape[1]
    tensor_count = lax.axis_size("etp")
    local_experts = gate_weight.shape[0]
    experts = local_experts * lax.axis_size("expert")
    group_tokens, group_routes, group_expo = (
        lax.all_gather(tokens, "etp", axis=0, tiled=True),
        lax.all_gather(routes[:, 0], "etp", axis=0, tiled=True),
        lax.all_gather(exponents, "etp", axis=0, tiled=True),
    )
    group_hidden = lax.all_to_all(hidden_grad, "etp", split_axis=1, concat_axis=0, tiled=True)
    group_size = group_tokens.shape[0]
    hidden_local = group_hidden.shape[1]
    capacity = max(2, 5 * group_size // (4 * experts))
    onehot = (group_routes[:, None] == jnp.arange(experts, dtype=jnp.int32)[None, :]).astype(
        jnp.int32
    )
    ranking = jnp.sum((jnp.cumsum(onehot, axis=0) - 1) * onehot, axis=1)
    slot_index = (group_routes * capacity + ranking).astype(jnp.int32)
    slot_owner = (
        jnp.full((experts * capacity,), group_size, jnp.int32)
        .at[slot_index]
        .set(jnp.arange(group_size, dtype=jnp.int32))
    )
    padded_tokens = jnp.concatenate(
        [group_tokens, jnp.zeros((1, feature_count), jnp.bfloat16)], axis=0
    )
    padded_hidden = jnp.concatenate(
        [group_hidden, jnp.zeros((1, hidden_local), jnp.bfloat16)], axis=0
    )
    padded_expo = jnp.concatenate([group_expo, jnp.zeros((1,), jnp.int32)], axis=0)
    packed_tokens = padded_tokens[slot_owner].reshape(experts, capacity, feature_count)
    packed_hidden = padded_hidden[slot_owner].reshape(experts, capacity, hidden_local)
    packed_expo = padded_expo[slot_owner].reshape(experts, capacity)
    quarter = feature_count // tensor_count
    packed_tokens = lax.dynamic_slice_in_dim(
        packed_tokens, lax.axis_index("etp") * quarter, quarter, 2
    )
    arrived_tokens = lax.all_to_all(
        packed_tokens, "expert", split_axis=0, concat_axis=0, tiled=True
    )
    arrived_hidden = lax.all_to_all(
        packed_hidden, "expert", split_axis=0, concat_axis=0, tiled=True
    )
    arrived_expo = lax.all_to_all(packed_expo, "expert", split_axis=0, concat_axis=0, tiled=True)
    arrived_tokens = lax.all_gather(arrived_tokens, "etp", axis=2, tiled=True)
    sources = arrived_tokens.shape[0] // local_experts
    slot_count = arrived_tokens.shape[1]
    tokens_split = arrived_tokens.reshape(sources, local_experts, slot_count, feature_count)
    hidden_split = arrived_hidden.reshape(sources, local_experts, slot_count, hidden_local)
    expo_split = arrived_expo.reshape(sources, local_experts, slot_count)
    gate_pre = jnp.einsum(
        "slmd,ldf->slmf", tokens_split, gate_weight, preferred_element_type=jnp.float32
    )
    up_pre = jnp.einsum(
        "slmd,ldf->slmf", tokens_split, up_weight, preferred_element_type=jnp.float32
    )
    scaled_grad = (
        hidden_split.astype(jnp.float32) * jnp.exp2(expo_split.astype(jnp.float32))[..., None]
    )
    sigmoid_gate = jax.nn.sigmoid(gate_pre)
    grad_gate = (
        scaled_grad * up_pre * sigmoid_gate * (1.0 + gate_pre * (1.0 - sigmoid_gate))
    ).astype(jnp.bfloat16)
    grad_up = (scaled_grad * gate_pre * sigmoid_gate).astype(jnp.bfloat16)
    partial_value = jnp.einsum(
        "slmf,ldf->slmd", grad_gate, gate_weight, preferred_element_type=jnp.float32
    )
    partial_value = partial_value + jnp.einsum(
        "slmf,ldf->slmd", grad_up, up_weight, preferred_element_type=jnp.float32
    )
    partial_value = partial_value.reshape(sources * local_experts, slot_count, feature_count)
    returned = lax.all_to_all(
        partial_value.astype(jnp.bfloat16), "expert", split_axis=0, concat_axis=0, tiled=True
    )
    token_rows = returned.reshape(experts * capacity, feature_count)[slot_index]
    result = lax.psum_scatter(
        token_rows.astype(jnp.float32).astype(jnp.bfloat16), "etp", scatter_dimension=0, tiled=True
    )
    return result


def solution(mesh):
    placed = (
        P(("expert", "etp"), None),
        P(("expert", "etp"), None),
        P(("expert", "etp"), None),
        P(("expert", "etp")),
        P("expert", None, "etp"),
        P("expert", None, "etp"),
    )
    return jax.shard_map(
        on_device, mesh=mesh, in_specs=placed, out_specs=P(("expert", "etp"), None), check_vma=False
    )
```

profile of v0, /device:TPU:1, one launch (start us, length us, event | category | flops | bytes accessed | tf_op | source)
XLA Modules:
  0.0 297.6 jit_solution(14542037688672506160)
XLA Ops:
  6.5 0.0 all-gather.5.cloned.1.call-start
  6.5 0.7 all-gather.5.cloned.1.call-update
  7.3 0.0 all-gather.7.cloned.1.call-start
  7.3 6.1 %all-gather = s32[512,1]{0,1:T(1,128)S(1)} all-gather(s32[128,1]{0,1:T(1,128)} %param.8), channel_id=2, replica_groups=mesh['expert'=8,'etp'=4] {'etp'}, dimensions={0}, use_global_device_ids=true | all-gather | bytes 2560 | tf_op jit(solution)/shard_map/all_gather | solution.py:14
  13.4 1.1 reduce-window.6
  14.5 0.2 slice_reduce_fusion
  14.8 0.1 fusion.29
  14.9 2.4 scatter_custom_fusion
  17.4 19.6 %all-gather.5.cloned.1.call-done = bf16[512,2560]{1,0:T(8,128)(2,1)} async-done(((bf16[128,2560]{1,0:T(8,128)(2,1)}), bf16[512,2560]{1,0:T(8,128)(2,1)}) %all-gather.5.cloned.1.call-update) | async-done | bytes 2621456 | tf_op jit(solution)/shard_map/all_gather | solution.py:13
  36.9 1.9 concatenate.11
  38.8 4.3 %gather_fusion.2 = bf16[640,2560]{1,0:T(8,128)(2,1)} fusion(bf16[513,2560]{1,0:T(8,128)(2,1)S(1)} %concatenate.11, s32[1024]{0:T(1024)S(1)} %pad_clamp_fusion.1), kind=kCustom, calls=%fused_computation.2 | custom fusion | bytes 6556160 | tf_op jit(solution)/shard_map/gather | solution.py:38
  43.2 0.0 copy-start
  43.2 1.3 constant_dynamic-slice_fusion
  44.5 25.9 %all_to_all.43 = bf16[8,80,640]{2,1,0:T(8,128)(2,1)} all-to-all(bf16[8,80,640]{2,1,0:T(8,128)(2,1)S(1)} %constant_dynamic-slice_fusion), channel_id=1, replica_groups=mesh['expert'=8,'etp'=4] {'expert'}, dimensions={0} | all-to-all | bytes 1638400 | tf_op jit(solution)/shard_map/all_to_all | solution.py:45
  70.4 0.0 copy-start.1
  70.4 0.0 all-gather.7.cloned.1.call-update
  70.5 0.0 copy-done
  70.5 1.0 copy.12
  71.5 5.2 %all-to-all-start = ((bf16[128,4,1024]{2,0,1:T(8,128)(2,1)}), bf16[128,4,1024]{2,0,1:T(8,128)(2,1)S(1)}, u32[]{:S(2)}, u32[]{:S(2)}) async-start(bf16[128,4,1024]{2,0,1:T(8,128)(2,1)} %bitcast.108), calls=%async_computation | async-start | bytes 2097152 | tf_op jit(solution)/shard_map/all_to_all | solution.py:17
  76.7 0.0 copy-done.1
  76.7 26.5 %all-gather.1 = s32[4,1,128]{2,1,0:T(1,128)S(1)} all-gather(s32[1,1,128]{2,1,0:T(1,128)S(1)} %bitcast.119), channel_id=1, replica_groups=mesh['expert'=8,'etp'=4] {'etp'}, dimensions={0}, use_global_device_ids=true | all-gather | bytes 2560 | tf_op jit(solution)/shard_map/all_gather | solution.py:15
  103.2 2.8 gather_fusion.1
  106.0 0.7 all_to_all.34
  106.7 0.0 all-to-all-done
  106.7 3.3 %all-to-all-start.2 = ((s32[8,1,80]{2,1,0:T(1,128)}), s32[8,1,80]{2,1,0:T(1,128)S(1)}, u32[]{:S(2)}, u32[]{:S(2)}) async-start(s32[8,1,80]{2,1,0:T(1,128)} %all_to_all.34), calls=%async_computation.2 | async-start | bytes 8192 | tf_op jit(solution)/shard_map/all_to_all | solution.py:51
  110.0 0.1 concatenate.9
  110.1 3.5 %gather_fusion = bf16[640,1024]{1,0:T(8,128)(2,1)} fusion(bf16[513,1024]{1,0:T(8,128)(2,1)S(1)} %concatenate.9, s32[1024]{0:T(1024)S(1)} %pad_clamp_fusion.1), kind=kCustom, calls=%fused_computation | custom fusion | bytes 2624000 | tf_op jit(solution)/shard_map/gather | solution.py:39
  113.6 1.7 all-to-all-done.2
  115.2 3.8 %all-to-all-start.1 = ((bf16[8,80,1024]{2,1,0:T(8,128)(2,1)}), bf16[8,80,1024]{2,1,0:T(8,128)(2,1)S(1)}, u32[]{:S(2)}, u32[]{:S(2)}) async-start(bf16[8,80,1024]{2,1,0:T(8,128)(2,1)} %bitcast.6), calls=%async_computation.1 | async-start | bytes 2621440 | tf_op jit(solution)/shard_map/all_to_all | solution.py:48
  119.0 0.0 all-gather.7.cloned.1.call-done
  119.0 8.5 %fusion.2 = f32[8,80,1024]{2,1,0:T(8,128)} fusion(bf16[8,80,2560]{2,1,0:T(8,128)(2,1)} %all-gather.7.cloned.1.call-done, bf16[1,2560,1024]{2,1,0:T(8,128)(2,1)} %param.10), kind=kOutput, calls=%fused_computation.8 | convolution fusion | flops 3355443200 | bytes 11141120 | tf_op jit(solution)/shard_map/slmd,ldf->slmf/dot_general | solution.py:58
  127.5 22.0 %all-to-all-done.1 = bf16[8,80,1024]{2,1,0:T(8,128)(2,1)S(1)} async-done(((bf16[8,80,1024]{2,1,0:T(8,128)(2,1)}), bf16[8,80,1024]{2,1,0:T(8,128)(2,1)S(1)}, u32[]{:S(2)}, u32[]{:S(2)}) %all-to-all-start.1) | async-done | bytes 1310752 | tf_op jit(solution)/shard_map/all_to_all | solution.py:48
  149.5 16.1 %fusion = f32[8,80,2560]{2,1,0:T(8,128)} fusion(bf16[1,2560,1024]{2,1,0:T(8,128)(2,1)} %param.10, f32[8,80,1024]{2,1,0:T(8,128)} %fusion.2, bf16[8,80,2560]{2,1,0:T(8,128)(2,1)} %all-gather.7.cloned.1.call-done, bf16[1,2560,1024]{2,1,0:T(8,128)(2,1)} %param.11, bf16[8,80,1024]{2,1,0:T(8,128)(2,1)S(1)} %all-to-all-done.1, f32[8,80]{1,0:T(8,128)S(1)} %bitcast.117), kind=kOutput, calls=%fused_computation.6 | convolution fusion | flops 6718750720 | bytes 24250880 | tf_op jit(solution)/shard_map/slmf,ldf->slmd/dot_general | solution.py:72
  165.6 10.9 %add_convert_fusion = bf16[8,80,2560]{2,1,0:T(8,128)(2,1)} fusion(f32[8,80,2560]{2,1,0:T(8,128)} %fusion, bf16[1,2560,1024]{2,1,0:T(8,128)(2,1)} %param.11, f32[8,80,1024]{2,1,0:T(8,128)} %fusion.2, bf16[8,80,1024]{2,1,0:T(8,128)(2,1)S(1)} %all-to-all-done.1, f32[8,80]{1,0:T(8,128)S(1)} %bitcast.118), kind=kOutput, calls=%fused_computation.5 | convolution fusion | flops 3363962880 | bytes 19008000 | tf_op jit(solution)/shard_map/slmf,ldf->slmd/dot_general | solution.py:75
  176.4 4.7 %all-to-all-start.4 = ((bf16[8,80,2560]{2,1,0:T(8,128)(2,1)}), bf16[8,80,2560]{2,1,0:T(8,128)(2,1)S(1)}, u32[]{:S(2)}, u32[]{:S(2)}) async-start(bf16[8,80,2560]{2,1,0:T(8,128)(2,1)} %add_convert_fusion), calls=%async_computation.4 | async-start | bytes 6553600 | tf_op jit(solution)/shard_map/all_to_all | solution.py:79
  181.1 0.0 reduce-scatter.2.cloned.1.call-start
  181.2 72.8 %all-to-all-done.4 = bf16[8,80,2560]{2,1,0:T(8,128)(2,1)S(1)} async-done(((bf16[8,80,2560]{2,1,0:T(8,128)(2,1)}), bf16[8,80,2560]{2,1,0:T(8,128)(2,1)S(1)}, u32[]{:S(2)}, u32[]{:S(2)}) %all-to-all-start.4) | async-done | bytes 3276832 | tf_op jit(solution)/shard_map/all_to_all | solution.py:79
  253.9 3.5 %gather_fusion.3 = bf16[512,2560]{1,0:T(8,128)(2,1)} fusion(bf16[640,2560]{1,0:T(8,128)(2,1)S(1)} %bitcast.109, s32[1024]{0:T(1024)S(1)} %pad_clamp_fusion), kind=kCustom, calls=%fused_computation.3 | custom fusion | bytes 5244928 | tf_op jit(solution)/shard_map/gather | solution.py:82
  257.5 0.0 reduce-scatter.2.cloned.1.call-update
  257.5 33.6 %reduce-scatter.2.cloned.1.call-done = bf16[128,2560]{1,0:T(8,128)(2,1)} async-done(((bf16[512,2560]{1,0:T(8,128)(2,1)}), bf16[128,2560]{1,0:T(8,128)(2,1)}) %reduce-scatter.2.cloned.1.call-update) | async-done | bytes 655376 | tf_op jit(solution)/shard_map/reduce_scatter | solution.py:83
  (10 shorter events, 0.1 us)
Async XLA Ops:
  6.5 30.4 %all-gather.5.cloned.1.call-start = ((), (), s32[]{:S(2)}) async-start(), calls=%async_computation.6 | async-start | bytes 3276800 | tf_op jit(solution)/shard_map/all_gather | solution.py:13
  7.3 111.8 %all-gather.7.cloned.1.call-start = ((), (), s32[]{:S(2)}) async-start(), calls=%async_computation.7 | async-start | bytes 4096000 | tf_op jit(solution)/shard_map/all_gather | solution.py:52
  43.2 27.3 %copy-start = (bf16[128,4096]{1,0:T(8,128)(2,1)S(1)}, bf16[128,4096]{1,0:T(8,128)(2,1)}, u32[]{:S(2)}) copy-start(bf16[128,4096]{1,0:T(8,128)(2,1)} %param.7) | copy-start | bytes 3145732
  70.4 6.3 %copy-start.1 = (s32[128]{0:T(128)S(1)}, s32[128]{0:T(128)}, u32[]{:S(2)}) copy-start(s32[128]{0:T(128)} %param.9) | copy-start | bytes 1540
  71.5 35.2 %all-to-all-start = ((bf16[128,4,1024]{2,0,1:T(8,128)(2,1)}), bf16[128,4,1024]{2,0,1:T(8,128)(2,1)S(1)}, u32[]{:S(2)}, u32[]{:S(2)}) async-start(bf16[128,4,1024]{2,0,1:T(8,128)(2,1)} %bitcast.108), calls=%async_computation | async-start | bytes 2097152 | tf_op jit(solution)/shard_map/all_to_all | solution.py:17
  106.7 8.5 %all-to-all-start.2 = ((s32[8,1,80]{2,1,0:T(1,128)}), s32[8,1,80]{2,1,0:T(1,128)S(1)}, u32[]{:S(2)}, u32[]{:S(2)}) async-start(s32[8,1,80]{2,1,0:T(1,128)} %all_to_all.34), calls=%async_computation.2 | async-start | bytes 8192 | tf_op jit(solution)/shard_map/all_to_all | solution.py:51
  115.2 34.3 %all-to-all-start.1 = ((bf16[8,80,1024]{2,1,0:T(8,128)(2,1)}), bf16[8,80,1024]{2,1,0:T(8,128)(2,1)S(1)}, u32[]{:S(2)}, u32[]{:S(2)}) async-start(bf16[8,80,1024]{2,1,0:T(8,128)(2,1)} %bitcast.6), calls=%async_computation.1 | async-start | bytes 2621440 | tf_op jit(solution)/shard_map/all_to_all | solution.py:48
  176.4 77.5 %all-to-all-start.4 = ((bf16[8,80,2560]{2,1,0:T(8,128)(2,1)}), bf16[8,80,2560]{2,1,0:T(8,128)(2,1)S(1)}, u32[]{:S(2)}, u32[]{:S(2)}) async-start(bf16[8,80,2560]{2,1,0:T(8,128)(2,1)} %add_convert_fusion), calls=%async_computation.4 | async-start | bytes 6553600 | tf_op jit(solution)/shard_map/all_to_all | solution.py:79
  181.1 109.9 %reduce-scatter.2.cloned.1.call-start = ((), (), s32[]{:S(2)}) async-start(), calls=%async_computation.8 | async-start | bytes 3276800 | tf_op jit(solution)/shard_map/reduce_scatter | solution.py:83
Sparse Core Ops, SparseCore 0:
  8.9 27.9 all-gather.4
  70.6 39.2 all-gather.6
  257.6 33.3 reduce-scatter.1
where the time goes:
time: 299 us; the launch traced here: 298 us
  waiting for transfers between devices  150 us (50%)
  blocking collectives  58.5 us (20%)
  matrix products  35.4 us (12%)
  local copies, waits for them, and re-layouts  21.8 us (7%)
  starting transfers between devices  17 us (6%)
  between operations  13.2 us (4%)
    all_to_all x1, waiting for transfers between devices, on_device(): lax.all_to_all(partial_value.astype(jnp.bfloat16), 'expert', split_axis=0...  72.8 us
    reduce_scatter x1, waiting for transfers between devices, on_device(): lax.psum_scatter(token_rows.astype(jnp.float32).astype(jnp.bfloat16), 'et...  33.6 us
    all_gather x1, blocking collectives, on_device(): lax.all_gather(exponents, 'etp', axis=0, tiled=True)  26.5 us
    all_to_all x1, blocking collectives, on_device(): lax.all_to_all(packed_tokens, 'expert', split_axis=0, concat_axis=0, tile...  25.9 us
    all_to_all x1, waiting for transfers between devices, on_device(): lax.all_to_all(packed_hidden, 'expert', split_axis=0, concat_axis=0, tile...  22 us
    all_gather x1, waiting for transfers between devices, on_device(): lax.all_gather(tokens, 'etp', axis=0, tiled=True)  19.6 us
    dot_general x1, matrix products, on_device(): jnp.einsum('slmf,ldf->slmd', grad_gate, gate_weight, preferred_element_ty...  16.1 us
    dot_general x1, matrix products, on_device(): jnp.einsum('slmf,ldf->slmd', grad_up, up_weight, preferred_element_type=j...  10.9 us
  transfers between devices with their start and end apart: 7, of which 5 were waited for; matrix products, arithmetic and copies ran while one was open for 7% of the time, Pallas kernels for 0%

commit v1 on v0

v1 whole, which is shorter than its diff:
```python
import functools

import jax
import jax.numpy as jnp
from jax import lax
from jax.experimental import pallas as pl
from jax.experimental.pallas import tpu as pltpu
from jax.sharding import PartitionSpec as P

MESH = pl.DeviceIdType.MESH
BF = jnp.bfloat16
F32 = jnp.float32


def flip(index, k, size):
    total, bit = 0, 1
    while bit < size:
        if (k // bit) % 2:
            total = total + bit * (1 - lax.rem(lax.div(index, bit), 2))
        else:
            total = total + bit * lax.rem(lax.div(index, bit), 2)
        bit *= 2
    return total


def quarter_of(p):
    return lax.rem(p, 2) * 2 + lax.div(p, 2)


def aligned(start, size, step=128):
    return pl.ds(pl.multiple_of(start, step), size)


def kernel(
    NE, NP, C, cap,
    meta, tok, hid, wg_hbm, wu_hbm, out,
    meta_rx, tok_rx, hid_rx, pm, pack_t, pack_h, full_t, arr_h, wg, wu, gg, gu,
    cs, ck, crx, xs, xrx, zs, ret, fs,
    loc, m_s, m_r, t_s, t_r, h_s, h_r, zt_s, zt_r, zh_s, zh_r, ag_s, ag_r,
    c_s, c_r, x_s, x_r, r_s, r_r, f_s, f_r,
):
    me_e, me_p = lax.axis_index("expert"), lax.axis_index("etp")
    B = NE // C
    M = B * cap
    T, D = tok.shape
    FL = wg.shape[1]
    Q, H = D // 4, D // 2
    TN = 256
    group = NP * T
    peers = [flip(me_p, j, NP) for j in range(NP)]
    far = [flip(me_e, k, NE) for k in range(NE)]
    my_cols = aligned(quarter_of(me_p) * Q, Q)

    def remote(src, dst, ss, rs, e, p):
        return pltpu.make_async_remote_copy(
            src_ref=src, dst_ref=dst, send_sem=ss, recv_sem=rs, device_id=(e, p), device_id_type=MESH
        )

    own_t = pltpu.make_async_copy(tok.at[:, my_cols], tok_rx.at[me_p], loc.at[0])
    own_h = pltpu.make_async_copy(hid.at[:, aligned(me_p * FL, FL)], hid_rx.at[me_p], loc.at[1])
    own_g = pltpu.make_async_copy(wg_hbm.at[0], wg, loc.at[2])
    own_u = pltpu.make_async_copy(wu_hbm.at[0], wu, loc.at[3])
    barrier = pltpu.get_barrier_semaphore()
    for j in range(1, NP):
        pl.semaphore_signal(barrier, inc=1, device_id=(me_e, peers[j]), device_id_type=MESH)
    for k in range(1, NE):
        pl.semaphore_signal(barrier, inc=1, device_id=(far[k], me_p), device_id_type=MESH)
    own_t.start()
    own_h.start()
    meta_rx[me_p] = meta[...]
    pl.semaphore_wait(barrier, NP - 1 + NE - 1)

    order = [2, 3, 1]
    started = []

    def go(copy):
        copy.start()
        started.append(copy)
        return copy

    metas = [go(remote(meta, meta_rx.at[me_p], m_s.at[j], m_r.at[j], me_e, peers[j])) for j in order]
    toks = [
        go(remote(tok.at[:, aligned(quarter_of(peers[j]) * Q, Q)], tok_rx.at[me_p], t_s.at[j], t_r.at[j], me_e, peers[j]))
        for j in order
    ]
    hids = [
        go(remote(hid.at[:, aligned(peers[j] * FL, FL)], hid_rx.at[me_p], h_s.at[j], h_r.at[j], me_e, peers[j]))
        for j in order
    ]
    own_g.start()
    own_u.start()

    for copy in metas:
        copy.wait_recv()
    route = jnp.concatenate([meta_rx[p][0:1, :] for p in range(NP)], axis=1)
    expo = jnp.concatenate([meta_rx[p][1:2, :] for p in range(NP)], axis=1)
    ids = lax.broadcasted_iota(jnp.int32, (NE, group), 0)
    onehot = jnp.where(ids == route, 1.0, 0.0)
    before = lax.broadcasted_iota(jnp.int32, (group, group), 0) <= lax.broadcasted_iota(jnp.int32, (group, group), 1)
    count = jnp.dot(onehot.astype(BF), jnp.where(before, 1.0, 0.0).astype(BF), preferred_element_type=F32)
    slot = jnp.sum(onehot * (ids.astype(F32) * cap + count - 1.0), axis=0, keepdims=True).astype(jnp.int32)
    scale = sum(jnp.where(expo == v, 2.0**v, 0.0) for v in range(-2, 3))
    rows = lax.broadcasted_iota(jnp.int32, (cap, group), 0)
    for c in range(C):
        for i in range(B):
            hit = jnp.where(rows + far[c * B + i] * cap == slot, 1.0, 0.0)
            pm[c, i * cap : (i + 1) * cap, :] = hit.astype(BF)

    own_t.wait()
    for copy in toks:
        copy.wait_recv()
    zts, zhs, rets = {}, {}, {}
    for c in range(C):
        block = jnp.dot(pm[c], tok_rx[...].reshape(group, Q), preferred_element_type=F32).astype(BF)
        pack_t[c] = block
        if c == 0:
            full_t[0, 0:cap, my_cols] = block[0:cap]
        for i in range(B):
            k = c * B + i
            if k:
                r = pl.ds(i * cap, cap)
                zts[k] = go(remote(pack_t.at[c, r], full_t.at[c, r, my_cols], zt_s.at[k], zt_r.at[k], far[k], me_p))
    own_h.wait()
    for copy in hids:
        copy.wait_recv()
    for c in range(C):
        scaled = (pm[c].astype(F32) * scale).astype(BF)
        block = jnp.dot(scaled, hid_rx[...].reshape(group, FL), preferred_element_type=F32).astype(BF)
        pack_h[c] = block
        if c == 0:
            arr_h[0, 0:cap, :] = block[0:cap]
        for i in range(B):
            k = c * B + i
            if k:
                r = pl.ds(i * cap, cap)
                zhs[k] = go(remote(pack_h.at[c, r], arr_h.at[c, r], zh_s.at[k], zh_r.at[k], far[k], me_p))

    their_cols = aligned(quarter_of(peers[2]) * Q, Q)
    spread = {}

    def share(c):
        for k in range(max(1, c * B), (c + 1) * B):
            zts[k].wait_recv()
        part = full_t.at[c, :, my_cols]
        spread[1, c] = go(remote(part, part, ag_s.at[1, c], ag_r.at[1, c], me_e, peers[2]))
        spread[0, c] = go(remote(part, part, ag_s.at[0, c], ag_r.at[0, c], me_e, peers[1]))

    def forward(c):
        spread[1, c].wait_recv()
        part = full_t.at[c, :, their_cols]
        spread[2, c] = go(remote(part, part, ag_s.at[2, c], ag_r.at[2, c], me_e, peers[1]))

    half = lax.rem(me_p, 2)
    side = lax.div(me_p, 2)
    nt = (((1,), (1,)), ((), ()))
    crossed, sided = {}, {}

    def compute(c):
        spread[0, c].wait_recv()
        spread[2, c].wait_recv()
        for k in range(max(1, c * B), (c + 1) * B):
            zhs[k].wait_recv()

        def first(n, carry):
            cols = aligned(n * TN, TN)
            x = full_t[c]
            gate = jnp.dot(x, wg[:, cols], preferred_element_type=F32)
            up = jnp.dot(x, wu[:, cols], preferred_element_type=F32)
            grad = arr_h[c, :, cols].astype(F32)
            s = 1.0 / (1.0 + jnp.exp(-gate))
            gg[:, cols] = (grad * up * s * (1.0 + gate * (1.0 - s))).astype(BF)
            gu[:, cols] = (grad * gate * s).astype(BF)
            return carry

        lax.fori_loop(0, FL // TN, first, 0)

        def back(start):
            r = aligned(start, TN)
            return lax.dot_general(gg[...], wg[r, :], nt, preferred_element_type=F32) + lax.dot_general(
                gu[...], wu[r, :], nt, preferred_element_type=F32
            )

        def give(t, carry):
            cs[c, :, aligned(t * TN, TN)] = back((1 - half) * H + t * TN).astype(BF)
            return carry

        def keep(t, carry):
            ck[c, :, aligned(t * TN, TN)] = back(half * H + t * TN)
            return carry

        lax.fori_loop(0, H // TN, give, 0)
        crossed[c] = go(remote(cs.at[c], crx.at[c], c_s.at[c], c_r.at[c], me_e, peers[1]))
        lax.fori_loop(0, H // TN, keep, 0)

    def x_step(c):
        crossed[c].wait_recv()
        cols = aligned((1 - side) * Q, Q)
        xs[c] = (ck[c, :, cols] + crx[c, :, cols].astype(F32)).astype(BF)
        sided[c] = go(remote(xs.at[c], xrx.at[c], x_s.at[c], x_r.at[c], me_e, peers[2]))

    def z_step(c):
        sided[c].wait_recv()
        cols = aligned(side * Q, Q)
        total = (ck[c, :, cols] + crx[c, :, cols].astype(F32) + xrx[c].astype(F32)).astype(BF)
        zs[c] = total
        if c == 0:
            ret[0, 0:cap, :] = total[0:cap]
        for i in range(B):
            k = c * B + i
            if k:
                r = pl.ds(i * cap, cap)
                rets[k] = go(remote(zs.at[c, r], ret.at[c, r], r_s.at[k], r_r.at[k], far[k], me_p))

    share(0)
    forward(0)
    if C > 1:
        share(1)
        forward(1)
    own_g.wait()
    own_u.wait()
    for c in range(C):
        if 0 < c < C - 1:
            share(c + 1)
            forward(c + 1)
        compute(c)
        if c >= 1:
            x_step(c - 1)
        if c >= 2:
            z_step(c - 2)
    x_step(C - 1)
    if C > 1:
        z_step(C - 2)
    z_step(C - 1)

    for k in range(1, NE):
        rets[k].wait_recv()
    tn = (((0,), (0,)), ((), ()))
    ends = []
    for j in order + [0]:
        cols = aligned(peers[j] * T, T)
        rows_j = sum(
            lax.dot_general(pm[c, :, cols], ret[c], tn, preferred_element_type=F32) for c in range(C)
        ).astype(BF)
        if j:
            fs[j] = rows_j
            ends.append(go(remote(fs.at[j], out.at[:, my_cols], f_s.at[j], f_r.at[j], me_e, peers[j])))
        else:
            out[:, my_cols] = rows_j
    for copy in ends:
        copy.wait_recv()
    for copy in started:
        copy.wait_send()


def on_device(NE, NP, tokens, hidden_grad, routes, exponents, gate_weight, up_weight):
    T, D = tokens.shape
    FL = gate_weight.shape[2]
    group = NP * T
    experts = NE * gate_weight.shape[0]
    cap = -(-max(2, 5 * group // (4 * experts)) // 16) * 16
    C = min(4, NE)
    M = NE // C * cap
    Q, H = D // 4, D // 2
    meta = jnp.concatenate(
        [routes[:, 0][None, :], exponents[None, :], jnp.zeros((6, T), jnp.int32)], axis=0
    )
    V = pltpu.VMEM
    dma = pltpu.SemaphoreType.DMA
    return pl.pallas_call(
        functools.partial(kernel, NE, NP, C, cap),
        out_shape=jax.ShapeDtypeStruct((T, D), BF),
        in_specs=[pl.BlockSpec(memory_space=V)] + [pl.BlockSpec(memory_space=pl.ANY)] * 4,
        out_specs=pl.BlockSpec(memory_space=V),
        scratch_shapes=[
            V((NP, 8, T), jnp.int32),
            V((NP, T, Q), BF),
            V((NP, T, FL), BF),
            V((C, M, group), BF),
            V((C, M, Q), BF),
            V((C, M, FL), BF),
            V((C, M, D), BF),
            V((C, M, FL), BF),
            V((D, FL), BF),
            V((D, FL), BF),
            V((M, FL), BF),
            V((M, FL), BF),
            V((C, M, H), BF),
            V((C, M, H), F32),
            V((C, M, H), BF),
            V((C, M, Q), BF),
            V((C, M, Q), BF),
            V((C, M, Q), BF),
            V((C, M, Q), BF),
            V((NP, T, Q), BF),
            dma((4,)),
            dma((NP,)), dma((NP,)), dma((NP,)), dma((NP,)), dma((NP,)), dma((NP,)),
            dma((NE,)), dma((NE,)), dma((NE,)), dma((NE,)),
            dma((3, C)), dma((3, C)),
            dma((C,)), dma((C,)), dma((C,)), dma((C,)),
            dma((NE,)), dma((NE,)),
            dma((NP,)), dma((NP,)),
        ],
        compiler_params=pltpu.CompilerParams(
            collective_id=0, has_side_effects=True, vmem_limit_bytes=60 * 1024 * 1024
        ),
    )(meta, tokens, hidden_grad, gate_weight, up_weight)


def solution(mesh):
    placed = (
        P(("expert", "etp"), None),
        P(("expert", "etp"), None),
        P(("expert", "etp"), None),
        P(("expert", "etp")),
        P("expert", None, "etp"),
        P("expert", None, "etp"),
    )
    body = functools.partial(on_device, mesh.shape["expert"], mesh.shape["etp"])
    return jax.shard_map(
        body, mesh=mesh, in_specs=placed, out_specs=P(("expert", "etp"), None), check_vma=False
    )
```

time: 299 us -> 121 us (0.40)
  the two profiles are of different devices: /device:TPU:1 before, /device:TPU:9 now
where the time goes in v1:
time: 121 us
  Pallas kernels  117 us (97%)
  local copies, waits for them, and re-layouts  2.04 us (2%)
  other arithmetic  1.33 us (1%)
    pallas_call x1, Pallas kernels, on_device(): pl.pallas_call(functools.partial(kernel, NE, NP, C, cap), out_shape=jax.S...  117 us

profile of v1, /device:TPU:9, one launch (start us, length us, event | category | flops | bytes accessed | tf_op | source)
XLA Modules:
  0.0 120.8 jit_solution(10938605422714456732)
XLA Ops:
  0.0 0.1 pad.2.clone
  0.1 1.3 %add_add_fusion.meta = s32[8,128]{1,0:T(8,128)} fusion(s32[1,128]{1,0:T(1,128)} %bitcast.2, s32[1,128]{1,0:T(1,128)} %bitcast.3, s32[8]{0:T(128)S(1)} %pad.2.clone), kind=kLoop, calls=%fused_computation | loop fusion | flops 2048 | bytes 5152 | tf_op jit(solution)/shard_map/concatenate | solution.py:264
  1.4 117.4 %shard_map.64 = bf16[128,2560]{1,0:T(8,128)(2,1)} custom-call(s32[8,128]{1,0:T(8,128)} %add_add_fusion.meta, bf16[128,2560]{1,0:T(8,128)(2,1)} %tok.1, bf16[128,4096]{1,0:T(8,128)(2,1)} %hid.1, bf16[1,2560,1024]{2,1,0:T(8,128)(2,1)} %wg_hbm.1, bf16[1,2560,1024]{2,1,0:T(8,128)(2,1)} %wu_hbm.1), custom_call_target="tpu_custom_call" | custom-call | tf_op jit(solution)/shard_map/pallas_call | solution.py:269
  118.8 2.0 %copy.8 = bf16[128,2560]{1,0:T(8,128)(2,1)} copy(bf16[128,2560]{1,0:T(8,128)(2,1)} %shard_map.64) | data formatting | bytes 1310720
  (1 shorter events, 0.0 us)

commit v2 on v1

v2 whole, which is shorter than its diff:
```python
import functools

import jax
import jax.numpy as jnp
from jax import lax
from jax.experimental import pallas as pl
from jax.experimental.pallas import tpu as pltpu
from jax.sharding import PartitionSpec as P

MESH = pl.DeviceIdType.MESH
BF = jnp.bfloat16
F32 = jnp.float32


def flip(index, k, size):
    total, bit = 0, 1
    while bit < size:
        if (k // bit) % 2:
            total = total + bit * (1 - lax.rem(lax.div(index, bit), 2))
        else:
            total = total + bit * lax.rem(lax.div(index, bit), 2)
        bit *= 2
    return total


def quarter_of(p):
    return lax.rem(p, 2) * 2 + lax.div(p, 2)


def aligned(start, size, step=128):
    return pl.ds(pl.multiple_of(start, step), size)


def kernel(
    NE, NP, C, cap,
    routes, expos, tok, hid, wg_hbm, wu_hbm, out,
    route_rx, expo_rx, tok_rx, hid_rx, pm, pack_t, pack_h, full_t, arr_h, wg, wu, gate_s, up_s, gg, gu,
    cs, ck, crx, xs, xrx, zs, ret, fs,
    loc, m_s, m_r, e_s, e_r, t_s, t_r, h_s, h_r, zt_s, zt_r, zh_s, zh_r, ag_s, ag_r,
    c_s, c_r, x_s, x_r, r_s, r_r, f_s, f_r,
):
    me_e, me_p = lax.axis_index("expert"), lax.axis_index("etp")
    B = NE // C
    M = B * cap
    T, D = tok.shape
    FL = wg.shape[1]
    Q, H = D // 4, D // 2
    TN = 256
    group = NP * T
    cut = max(128, Q // 256 * 128)
    pieces = [(0, cut), (cut, Q - cut)]
    peers = [flip(me_p, j, NP) for j in range(NP)]
    far = [flip(me_e, k, NE) for k in range(NE)]
    my_base = quarter_of(me_p) * Q
    my_cols = aligned(my_base, Q)

    def remote(src, dst, ss, rs, e, p):
        return pltpu.make_async_remote_copy(
            src_ref=src, dst_ref=dst, send_sem=ss, recv_sem=rs, device_id=(e, p), device_id_type=MESH
        )

    own_t = pltpu.make_async_copy(tok.at[:, my_cols], tok_rx.at[me_p], loc.at[0])
    own_h = pltpu.make_async_copy(hid.at[:, aligned(me_p * FL, FL)], hid_rx.at[me_p], loc.at[1])
    own_g = pltpu.make_async_copy(wg_hbm.at[0], wg, loc.at[2])
    own_u = pltpu.make_async_copy(wu_hbm.at[0], wu, loc.at[3])
    barrier = pltpu.get_barrier_semaphore()
    for j in range(1, NP):
        pl.semaphore_signal(barrier, inc=1, device_id=(me_e, peers[j]), device_id_type=MESH)
    for k in range(1, NE):
        pl.semaphore_signal(barrier, inc=1, device_id=(far[k], me_p), device_id_type=MESH)
    own_t.start()
    own_h.start()
    route_rx[me_p] = routes[...]
    expo_rx[me_p] = expos[...]
    pl.semaphore_wait(barrier, NP - 1 + NE - 1)

    order = [2, 3, 1]
    started = []

    def go(copy):
        copy.start()
        started.append(copy)
        return copy

    metas = [go(remote(routes, route_rx.at[me_p], m_s.at[j], m_r.at[j], me_e, peers[j])) for j in order]
    metas += [go(remote(expos, expo_rx.at[me_p], e_s.at[j], e_r.at[j], me_e, peers[j])) for j in order]
    toks = [
        [
            go(remote(
                tok.at[:, aligned(quarter_of(peers[j]) * Q + lo, n)], tok_rx.at[me_p, :, pl.ds(lo, n)],
                t_s.at[s, j], t_r.at[s, j], me_e, peers[j],
            ))
            for j in order
        ]
        for s, (lo, n) in enumerate(pieces)
    ]
    hids = [
        go(remote(hid.at[:, aligned(peers[j] * FL, FL)], hid_rx.at[me_p], h_s.at[j], h_r.at[j], me_e, peers[j]))
        for j in order
    ]
    own_g.start()
    own_u.start()

    for copy in metas:
        copy.wait_recv()
    route = jnp.concatenate([route_rx[p] for p in range(NP)], axis=1)
    expo = jnp.concatenate([expo_rx[p] for p in range(NP)], axis=1)
    ids = lax.broadcasted_iota(jnp.int32, (NE, group), 0)
    onehot = jnp.where(ids == route, 1.0, 0.0)
    before = lax.broadcasted_iota(jnp.int32, (group, group), 0) <= lax.broadcasted_iota(jnp.int32, (group, group), 1)
    count = jnp.dot(onehot.astype(BF), jnp.where(before, 1.0, 0.0).astype(BF), preferred_element_type=F32)
    slot = jnp.sum(onehot * (ids.astype(F32) * cap + count - 1.0), axis=0, keepdims=True).astype(jnp.int32)
    scale = sum(jnp.where(expo == v, 2.0**v, 0.0) for v in range(-2, 3))
    rows = lax.broadcasted_iota(jnp.int32, (cap, group), 0)
    for c in range(C):
        for i in range(B):
            hit = jnp.where(rows + far[c * B + i] * cap == slot, 1.0, 0.0)
            pm[c, i * cap : (i + 1) * cap, :] = hit.astype(BF)

    own_t.wait()
    zts, zhs, rets = {}, {}, {}
    for s, (lo, n) in enumerate(pieces):
        for copy in toks[s]:
            copy.wait_recv()
        for c in range(C):
            piece = tok_rx[:, :, lo : lo + n].reshape(group, n)
            block = jnp.dot(pm[c], piece, preferred_element_type=F32).astype(BF)
            pack_t[c, :, lo : lo + n] = block
            cols = aligned(my_base + lo, n)
            if c == 0:
                full_t[0, 0:cap, cols] = block[0:cap]
            for i in range(B):
                k = c * B + i
                if k:
                    r = pl.ds(i * cap, cap)
                    zts[k, s] = go(remote(
                        pack_t.at[c, r, pl.ds(lo, n)], full_t.at[c, r, cols], zt_s.at[s, k], zt_r.at[s, k], far[k], me_p
                    ))
    own_h.wait()
    for copy in hids:
        copy.wait_recv()
    for c in ([2, 3, 0, 1] if C == 4 else range(C)):
        scaled = (pm[c].astype(F32) * scale).astype(BF)
        block = jnp.dot(scaled, hid_rx[...].reshape(group, FL), preferred_element_type=F32).astype(BF)
        pack_h[c] = block
        if c == 0:
            arr_h[0, 0:cap, :] = block[0:cap]
        for i in range(B):
            k = c * B + i
            if k:
                r = pl.ds(i * cap, cap)
                zhs[k] = go(remote(pack_h.at[c, r], arr_h.at[c, r], zh_s.at[k], zh_r.at[k], far[k], me_p))

    their_cols = aligned(quarter_of(peers[2]) * Q, Q)
    spread = {}

    def share(c):
        for k in range(max(1, c * B), (c + 1) * B):
            zts[k, 0].wait_recv()
            zts[k, 1].wait_recv()
        part = full_t.at[c, :, my_cols]
        spread[1, c] = go(remote(part, part, ag_s.at[1, c], ag_r.at[1, c], me_e, peers[2]))
        spread[0, c] = go(remote(part, part, ag_s.at[0, c], ag_r.at[0, c], me_e, peers[1]))

    def forward(c):
        spread[1, c].wait_recv()
        part = full_t.at[c, :, their_cols]
        spread[2, c] = go(remote(part, part, ag_s.at[2, c], ag_r.at[2, c], me_e, peers[1]))

    half = lax.rem(me_p, 2)
    side = lax.div(me_p, 2)
    nt = (((1,), (1,)), ((), ()))
    crossed, sided = {}, {}
    tiles = H // TN
    lead = -(-Q // TN)
    sent_q, kept_q = (1 - side) * Q, side * Q

    def tile_at(t):
        return (side * t + (1 - side) * (tiles - 1 - t)) * TN

    def forth(c):
        spread[0, c].wait_recv()
        spread[2, c].wait_recv()

        def step(n, carry):
            cols = aligned(n * TN, TN)
            x = full_t[c]
            gate_s[c, :, cols] = jnp.dot(x, wg[:, cols], preferred_element_type=F32)
            up_s[c, :, cols] = jnp.dot(x, wu[:, cols], preferred_element_type=F32)
            return carry

        lax.fori_loop(0, FL // TN, step, 0)

    def back(c, between=None):
        for k in range(max(1, c * B), (c + 1) * B):
            zhs[k].wait_recv()

        def act(n, carry):
            cols = aligned(n * TN, TN)
            gate, up = gate_s[c, :, cols], up_s[c, :, cols]
            grad = arr_h[c, :, cols].astype(F32)
            s = 1.0 / (1.0 + jnp.exp(-gate))
            gg[:, cols] = (grad * up * s * (1.0 + gate * (1.0 - s))).astype(BF)
            gu[:, cols] = (grad * gate * s).astype(BF)
            return carry

        lax.fori_loop(0, FL // TN, act, 0)

        def product(start):
            r = aligned(start, TN)
            return lax.dot_general(gg[...], wg[r, :], nt, preferred_element_type=F32) + lax.dot_general(
                gu[...], wu[r, :], nt, preferred_element_type=F32
            )

        def give(t, carry):
            cs[c, :, aligned(tile_at(t), TN)] = product((1 - half) * H + tile_at(t)).astype(BF)
            return carry

        def keep(t, carry):
            ck[c, :, aligned(tile_at(t), TN)] = product(half * H + tile_at(t))
            return carry

        def cross(q, base):
            part = pl.ds(pl.multiple_of(base, 128), Q)
            crossed[q, c] = go(remote(
                cs.at[c, :, part], crx.at[c, :, part], c_s.at[q, c], c_r.at[q, c], me_e, peers[1]
            ))

        lax.fori_loop(0, lead, give, 0)
        cross(0, sent_q)
        lax.fori_loop(lead, tiles, give, 0)
        cross(1, kept_q)
        lax.fori_loop(0, lead, keep, 0)
        crossed[0, c].wait_recv()
        for s, (lo, n) in enumerate(pieces):
            cols = aligned(sent_q + lo, n)
            here = pl.ds(lo, n)
            xs[c, :, here] = (ck[c, :, cols] + crx[c, :, cols].astype(F32)).astype(BF)
            sided[s, c] = go(remote(
                xs.at[c, :, here], xrx.at[c, :, here], x_s.at[s, c], x_r.at[s, c], me_e, peers[2]
            ))
        if between is not None:
            between()
        lax.fori_loop(lead, tiles, keep, 0)

    def z_step(c):
        crossed[1, c].wait_recv()
        for s, (lo, n) in enumerate(pieces):
            sided[s, c].wait_recv()
            cols = aligned(kept_q + lo, n)
            here = pl.ds(lo, n)
            total = (ck[c, :, cols] + crx[c, :, cols].astype(F32) + xrx[c, :, here].astype(F32)).astype(BF)
            zs[c, :, here] = total
            if c == 0:
                ret[0, 0:cap, here] = total[0:cap]
            for i in range(B):
                k = c * B + i
                if k:
                    r = pl.ds(i * cap, cap)
                    rets[k, s] = go(remote(
                        zs.at[c, r, here], ret.at[c, r, here], r_s.at[s, k], r_r.at[s, k], far[k], me_p
                    ))

    def gather(c):
        share(c)
        forward(c)

    if C == 4:
        gather(0)
        gather(1)
        own_g.wait()
        own_u.wait()
        forth(0)
        gather(2)
        forth(1)
        gather(3)
        forth(2)
        forth(3)
        back(2)
        back(0)
        z_step(2)
        back(3)
        z_step(0)
        back(1, lambda: z_step(3))
        z_step(1)
    else:
        own_g.wait()
        own_u.wait()
        for c in range(C):
            gather(c)
            forth(c)
            back(c)
            z_step(c)

    tn = (((0,), (0,)), ((), ()))
    ends = []
    for s, (lo, n) in enumerate(pieces):
        for k in range(1, NE):
            rets[k, s].wait_recv()
        here = pl.ds(lo, n)
        cols = aligned(my_base + lo, n)
        piece = ret[:, :, lo : lo + n].reshape(C * M, n)
        for j in order + [0]:
            pick = pm[:, :, aligned(peers[j] * T, T)].reshape(C * M, T)
            rows_j = lax.dot_general(pick, piece, tn, preferred_element_type=F32).astype(BF)
            if j:
                fs[j, :, here] = rows_j
                ends.append(go(remote(fs.at[j, :, here], out.at[:, cols], f_s.at[s, j], f_r.at[s, j], me_e, peers[j])))
            else:
                out[:, cols] = rows_j
    for copy in ends:
        copy.wait_recv()
    for copy in started:
        copy.wait_send()


def on_device(NE, NP, tokens, hidden_grad, routes, exponents, gate_weight, up_weight):
    T, D = tokens.shape
    FL = gate_weight.shape[2]
    group = NP * T
    experts = NE * gate_weight.shape[0]
    cap = -(-max(2, 5 * group // (4 * experts)) // 16) * 16
    C = min(4, NE)
    M = NE // C * cap
    Q, H = D // 4, D // 2
    V = pltpu.VMEM
    dma = pltpu.SemaphoreType.DMA
    return pl.pallas_call(
        functools.partial(kernel, NE, NP, C, cap),
        out_shape=jax.ShapeDtypeStruct((T, D), BF),
        in_specs=[pl.BlockSpec(memory_space=V)] * 2 + [pl.BlockSpec(memory_space=pl.ANY)] * 4,
        out_specs=pl.BlockSpec(memory_space=V),
        scratch_shapes=[
            V((NP, 1, T), jnp.int32),
            V((NP, 1, T), jnp.int32),
            V((NP, T, Q), BF),
            V((NP, T, FL), BF),
            V((C, M, group), BF),
            V((C, M, Q), BF),
            V((C, M, FL), BF),
            V((C, M, D), BF),
            V((C, M, FL), BF),
            V((D, FL), BF),
            V((D, FL), BF),
            V((C, M, FL), F32),
            V((C, M, FL), F32),
            V((M, FL), BF),
            V((M, FL), BF),
            V((C, M, H), BF),
            V((C, M, H), F32),
            V((C, M, H), BF),
            V((C, M, Q), BF),
            V((C, M, Q), BF),
            V((C, M, Q), BF),
            V((C, M, Q), BF),
            V((NP, T, Q), BF),
            dma((4,)),
            dma((NP,)), dma((NP,)), dma((NP,)), dma((NP,)),
            dma((2, NP)), dma((2, NP)), dma((NP,)), dma((NP,)),
            dma((2, NE)), dma((2, NE)), dma((NE,)), dma((NE,)),
            dma((3, C)), dma((3, C)),
            dma((2, C)), dma((2, C)), dma((2, C)), dma((2, C)),
            dma((2, NE)), dma((2, NE)),
            dma((2, NP)), dma((2, NP)),
        ],
        compiler_params=pltpu.CompilerParams(
            collective_id=0, has_side_effects=True, vmem_limit_bytes=60 * 1024 * 1024
        ),
    )(routes.reshape(1, T), exponents.reshape(1, T), tokens, hidden_grad, gate_weight, up_weight)


def solution(mesh):
    placed = (
        P(("expert", "etp"), None),
        P(("expert", "etp"), None),
        P(("expert", "etp"), None),
        P(("expert", "etp")),
        P("expert", None, "etp"),
        P("expert", None, "etp"),
    )
    body = functools.partial(on_device, mesh.shape["expert"], mesh.shape["etp"])
    return jax.shard_map(
        body, mesh=mesh, in_specs=placed, out_specs=P(("expert", "etp"), None), check_vma=False
    )
```

time: 121 us -> 107 us (0.88)
  the two profiles are of different devices: /device:TPU:9 before, /device:TPU:1 now
where the time goes in v2:
time: 107 us
  Pallas kernels  105 us (98%)
  local copies, waits for them, and re-layouts  1.97 us (2%)
    pallas_call x1, Pallas kernels, on_device(): pl.pallas_call(functools.partial(kernel, NE, NP, C, cap), out_shape=jax.S...  105 us

profile of v2, /device:TPU:1, one launch (start us, length us, event | category | flops | bytes accessed | tf_op | source)
XLA Modules:
  0.0 106.8 jit_solution(7129637855675291718)
XLA Ops:
  0.0 104.8 %shard_map.64 = bf16[128,2560]{1,0:T(8,128)(2,1)} custom-call(s32[1,128]{1,0:T(1,128)} %bitcast.2, s32[1,128]{1,0:T(1,128)} %bitcast.3, bf16[128,2560]{1,0:T(8,128)(2,1)} %tok.1, bf16[128,4096]{1,0:T(8,128)(2,1)} %hid.1, bf16[1,2560,1024]{2,1,0:T(8,128)(2,1)} %wg_hbm.1, bf16[1,2560,1024]{2,1,0:T(8,128)(2,1)} %wu_hbm.1), custom_call_target="tpu_custom_call" | custom-call | tf_op jit(solution)/shard_map/pallas_call | solution.py:328
  104.8 2.0 %copy.8 = bf16[128,2560]{1,0:T(8,128)(2,1)} copy(bf16[128,2560]{1,0:T(8,128)(2,1)} %shard_map.64) | data formatting | bytes 1310720

commit v3 on v2

--- a/solution.py
+++ b/solution.py
@@ -34,7 +34,7 @@
 def kernel(
     NE, NP, C, cap,
     routes, expos, tok, hid, wg_hbm, wu_hbm, out,
-    route_rx, expo_rx, tok_rx, hid_rx, pm, pack_t, pack_h, full_t, arr_h, wg, wu, gate_s, up_s, gg, gu,
+    route_rx, expo_rx, tok_rx, hid_rx, pm, pack_t, pack_h, full_t, arr_h, wg, wu, wgt, wut, gate_s, up_s, gg, gu,
     cs, ck, crx, xs, xrx, zs, ret, fs,
     loc, m_s, m_r, e_s, e_r, t_s, t_r, h_s, h_r, zt_s, zt_r, zh_s, zh_r, ag_s, ag_r,
     c_s, c_r, x_s, x_r, r_s, r_r, f_s, f_r,
@@ -136,6 +136,16 @@
                     zts[k, s] = go(remote(
                         pack_t.at[c, r, pl.ds(lo, n)], full_t.at[c, r, cols], zt_s.at[s, k], zt_r.at[s, k], far[k], me_p
                     ))
+    own_g.wait()
+    own_u.wait()
+
+    def turn(n, carry):
+        r = aligned(n * TN, TN)
+        wgt[:, r] = wg[r, :].T
+        wut[:, r] = wu[r, :].T
+        return carry
+
+    lax.fori_loop(0, D // TN, turn, 0)
     own_h.wait()
     for copy in hids:
         copy.wait_recv()
@@ -169,7 +179,6 @@
 
     half = lax.rem(me_p, 2)
     side = lax.div(me_p, 2)
-    nt = (((1,), (1,)), ((), ()))
     crossed, sided = {}, {}
     tiles = H // TN
     lead = -(-Q // TN)
@@ -208,8 +217,8 @@
 
         def product(start):
             r = aligned(start, TN)
-            return lax.dot_general(gg[...], wg[r, :], nt, preferred_element_type=F32) + lax.dot_general(
-                gu[...], wu[r, :], nt, preferred_element_type=F32
+            return jnp.dot(gg[...], wgt[:, r], preferred_element_type=F32) + jnp.dot(
+                gu[...], wut[:, r], preferred_element_type=F32
             )
 
         def give(t, carry):
@@ -268,8 +277,6 @@
     if C == 4:
         gather(0)
         gather(1)
-        own_g.wait()
-        own_u.wait()
         forth(0)
         gather(2)
         forth(1)
@@ -284,8 +291,6 @@
         back(1, lambda: z_step(3))
         z_step(1)
     else:
-        own_g.wait()
-        own_u.wait()
         for c in range(C):
             gather(c)
             forth(c)
@@ -342,6 +347,8 @@
             V((C, M, FL), BF),
             V((D, FL), BF),
             V((D, FL), BF),
+            V((FL, D), BF),
+            V((FL, D), BF),
             V((C, M, FL), F32),
             V((C, M, FL), F32),
             V((M, FL), BF),

time: 107 us -> 103 us (0.963)
  Pallas kernels: 105 us -> 101 us
    pallas_call x1, Pallas kernels: 105 us -> 101 us  [on_device(): pl.pallas_call(functools.partial(kernel, NE, NP, C, cap), out_shape=jax.S...]
where the time goes in v3:
time: 103 us
  Pallas kernels  101 us (98%)
  local copies, waits for them, and re-layouts  1.97 us (2%)
    pallas_call x1, Pallas kernels, on_device(): pl.pallas_call(functools.partial(kernel, NE, NP, C, cap), out_shape=jax.S...  101 us

profile of v3, /device:TPU:1, one launch (start us, length us, event | category | flops | bytes accessed | tf_op | source)
XLA Modules:
  0.0 102.5 jit_solution(17799156900213904768)
XLA Ops:
  0.0 100.5 %shard_map.64 = bf16[128,2560]{1,0:T(8,128)(2,1)} custom-call(s32[1,128]{1,0:T(1,128)} %bitcast.2, s32[1,128]{1,0:T(1,128)} %bitcast.3, bf16[128,2560]{1,0:T(8,128)(2,1)} %tok.1, bf16[128,4096]{1,0:T(8,128)(2,1)} %hid.1, bf16[1,2560,1024]{2,1,0:T(8,128)(2,1)} %wg_hbm.1, bf16[1,2560,1024]{2,1,0:T(8,128)(2,1)} %wu_hbm.1), custom_call_target="tpu_custom_call" | custom-call | tf_op jit(solution)/shard_map/pallas_call | solution.py:333
  100.6 2.0 %copy.8 = bf16[128,2560]{1,0:T(8,128)(2,1)} copy(bf16[128,2560]{1,0:T(8,128)(2,1)} %shard_map.64) | data formatting | bytes 1310720
